TPU v7x, 32 devices: a whole 2x2x4 slice. The times are simulated.
32 devices in a mesh: mem: 8 (over z, core), slab: 4 (over y, x).
Axes of the slice: x: 2, y: 2, z: 4, core: 2. Of those that a mesh axis runs over, the one named last changes fastest.
Arguments:
- thickness: float32 [64, 256, 384], P('mem', 'slab'), may hold values from 0.5 to 2.5
- face_u: float32 [256, 384], P('slab'), may hold values from -0.4 to 0.4
- face_v: float32 [256, 384], P('slab'), may hold values from -0.4 to 0.4
- obs_cells: int32 [512, 4], P('slab'), may hold values from 0 to 98303, as said below
- obs_weights: int32 [512, 4], P('slab'), may hold values from 1 to 4
- obs_values: float32 [512], P('slab'), may hold values from -6 to 6
- obs_noise: float32 [64, 512], P('mem', 'slab'), may hold values from -3 to 3
- cov_inverse: float32 [512, 512], P('slab'), may hold values from -0.375 to 0.375
- taper_mask: int32 [4, 4], replicated, may hold values from 0 to 1, as said below
Outputs:
- analysis: float32 [64, 256, 384], P('mem', 'slab')
Inputs may be any that keep to these rules, and one draw needn't show every extreme that they name: `obs_cells`: observation o covers a 2 x 2 square of cells, all within the rows of slab o // 128. `taper_mask`: entries are 0 or 1 and the diagonal is 1.
All inputs are finite; a program needn't handle non-finite values.
Results may differ from a plain program's by a relative error of at most 0.0003.
Values sent between devices are 32-bit elements; how exact they have to be, the bound alone decides.
A program may use at most 64 MiB of HBM per device.

v0:
```python
import jax
import jax.numpy as jnp
from jax import lax
from jax.sharding import PartitionSpec as P


def padded_2(block, sides, width):
    for axis, dim in sides:
        count = lax.axis_size(axis)
        forward = [(i, i + 1) for i in range(count - 1)]
        backward = [(target, source) for source, target in forward]
        low = lax.ppermute(
            lax.slice_in_dim(block, block.shape[dim] - width, None, axis=dim), axis, forward
        )
        high = lax.ppermute(lax.slice_in_dim(block, 0, width, axis=dim), axis, backward)
        block = jnp.concatenate([low, block, high], axis=dim)
    return block


def minmod(first_diff, second_diff):
    return (
        0.5
        * (jnp.sign(first_diff) + jnp.sign(second_diff))
        * jnp.minimum(jnp.abs(first_diff), jnp.abs(second_diff))
    )


def face_flux(padded, velocity, axis_dim):
    counted = padded.shape[axis_dim] - 3
    far_low = lax.slice_in_dim(padded, 0, counted, axis=axis_dim)
    near_low = lax.slice_in_dim(padded, 1, 1 + counted, axis=axis_dim)
    near_high = lax.slice_in_dim(padded, 2, 2 + counted, axis=axis_dim)
    far_high = lax.slice_in_dim(padded, 3, 3 + counted, axis=axis_dim)
    left_state = near_low + 0.5 * minmod(near_low - far_low, near_high - near_low)
    right_state = near_high - 0.5 * minmod(near_high - near_low, far_high - near_high)
    return jnp.maximum(velocity, 0.0) * left_state + jnp.minimum(velocity, 0.0) * right_state


def local(
    thickness,
    face_u,
    face_v,
    obs_cells,
    obs_weights,
    obs_values,
    obs_noise,
    cov_inverse,
    taper_mask,
):
    member_subset = thickness.shape[0]
    band_rows = thickness.shape[1]
    column_list = thickness.shape[2]
    slab_index = lax.axis_index("slab")
    stacked = jnp.concatenate([thickness, face_v[None]], 0)
    padded = padded_2(stacked, (("slab", 1),), 2)
    row_pad = padded[:member_subset]
    row_speed = padded[member_subset, 2 : band_rows + 3]
    row_fluxes = face_flux(row_pad, row_speed, 1)
    col_pad = jnp.pad(thickness, ((0, 0), (0, 0), (2, 2)))
    col_speed = jnp.pad(face_u, ((0, 0), (0, 1)))
    column_fluxes = face_flux(col_pad, col_speed, 2)
    prior_state = (
        thickness
        - (column_fluxes[:, :, 1:] - column_fluxes[:, :, :-1])
        - (row_fluxes[:, 1:, :] - row_fluxes[:, :-1, :])
    )
    state_vector = prior_state.reshape(member_subset, band_rows * column_list)
    local_cells = obs_cells - slab_index * (band_rows * column_list)
    weights = obs_weights.astype(jnp.float32)
    picked = state_vector[:, local_cells]
    obs_model = jnp.sum(picked * weights[None], -1) / jnp.sum(weights, -1)[None]
    innovation = obs_values[None, :] + obs_noise - obs_model
    white_terms = jnp.dot(innovation, cov_inverse, precision=lax.Precision.HIGHEST)
    whitened = lax.psum_scatter(white_terms, "slab", scatter_dimension=1, tiled=True)
    model_all, white_all = (
        lax.all_gather(obs_model, "mem", axis=0, tiled=True),
        lax.all_gather(whitened, "mem", axis=0, tiled=True),
    )
    obs_mean = jnp.mean(model_all, 0, keepdims=True)
    cell_state = lax.all_to_all(state_vector, "mem", split_axis=1, concat_axis=0, tiled=True)
    members = cell_state.shape[0]
    anomaly = cell_state - jnp.mean(cell_state, 0, keepdims=True)
    obs_anomaly = model_all - obs_mean
    anom_full, white_full = (
        lax.all_gather(obs_anomaly, "slab", axis=1, tiled=True),
        lax.all_gather(white_all, "slab", axis=1, tiled=True),
    )
    block_size = obs_anomaly.shape[1]
    mask_row = lax.dynamic_slice_in_dim(taper_mask, slab_index, 1, 0)[0].astype(jnp.float32)
    taper_row = jnp.repeat(mask_row, block_size)
    cross = lax.dot_general(
        anomaly, anom_full, (((0,), (0,)), ((), ())), precision=lax.Precision.HIGHEST
    ) / (members - 1)
    tapered = cross * taper_row[None, :]
    update = lax.dot_general(
        white_full, tapered, (((1,), (1,)), ((), ())), precision=lax.Precision.HIGHEST
    )
    analysis_cells = cell_state + update
    returned = lax.all_to_all(analysis_cells, "mem", split_axis=0, concat_axis=1, tiled=True)
    return returned.reshape(member_subset, band_rows, column_list)


def solution(mesh):
    return jax.shard_map(
        local,
        mesh=mesh,
        in_specs=(
            P("mem", "slab", None),
            P("slab", None),
            P("slab", None),
            P("slab", None),
            P("slab", None),
            P("slab"),
            P("mem", "slab"),
            P("slab", None),
            P(),
        ),
        out_specs=P("mem", "slab", None),
        check_vma=False,
    )
```

profile of v0, /device:TPU:0, one launch (start us, length us, event | category | flops | bytes accessed | tf_op | source)
XLA Modules:
  0.0 138.8 jit_solution(13175700690734752969)
XLA Ops:
  6.5 1.1 pad_maximum_fusion.3
  7.6 1.3 collective-permute-start
  8.9 5.5 %collective-permute-start.1 = (f32[9,2,384]{2,1,0:T(2,128)S(1)}, f32[9,2,384]{2,1,0:T(2,128)S(1)}, u32[]{:S(2)}, u32[]{:S(2)}) collective-permute-start(f32[9,2,384]{2,1,0:T(2,128)S(1)} %get-tuple-element.9), channel_id=1, source_target_pairs={{0,1},{1,2},{2,3},{4,5},{5,6},{6,7},{8,9},{9,10},{10,11},{12,13},{... | collective-permute-start | bytes 82952 | tf_op jit(solution)/shard_map/ppermute | solution.py:12
  14.4 0.9 pad_maximum_fusion.1
  15.4 0.7 compare_select_fusion
  16.1 0.1 copy.36
  16.2 0.1 reshape.37
  16.3 3.6 %multiply_add_fusion = f32[8,64,385]{2,1,0:T(8,128)S(1)} fusion(f32[8,64,384]{2,1,0:T(8,128)} %param.9, f32[64,385]{1,0:T(8,128)S(1)} %get-tuple-element.12, f32[64,385]{1,0:T(8,128)S(1)} %get-tuple-element.11), kind=kLoop, calls=%fused_computation.12 | loop fusion | flops 4730880 | bytes 1772032 | tf_op jit(solution)/shard_map/add | solution.py:36
  19.9 0.7 convert_reduce_fusion
  20.6 0.9 maximum_bitcast_fusion
  21.6 1.6 %maximum_maximum_fusion = (f32[9,66,384]{2,1,0:T(8,128)S(1)}, f32[9,66,384]{2,1,0:T(8,128)S(1)}) fusion(f32[1,64,384]{2,1,0:T(8,128)} %bitcast.30, f32[8,64,384]{2,1,0:T(8,128)} %param.9, f32[9,2,384]{2,1,0:T(2,128)S(1)} %collective-permute-done.1, f32[9,2,384]{2,1,0:T(2,128)S(1)} %collective-permute-done), kind=kLoop, calls=%fused_computation.14 | loop fusion | flops 912384 | bytes 2764800 | tf_op jit(solution)/shard_map/concatenate | solution.py:16
  23.2 1.3 multiply_add_fusion.1
  24.5 0.3 fusion.11
  24.9 0.1 all_to_all.26
  25.0 1.3 copy.34
  26.4 5.4 %all-to-all-start = ((f32[8,8,3072]{2,0,1:T(8,128)}), f32[8,8,3072]{2,0,1:T(8,128)S(1)}, u32[]{:S(2)}, u32[]{:S(2)}) async-start(f32[8,8,3072]{2,0,1:T(8,128)} %copy.34), calls=%async_computation | async-start | bytes 1572864 | tf_op jit(solution)/shard_map/all_to_all | solution.py:80
  31.8 0.7 multiply_bitcast_fusion
  32.5 0.1 copy.37
  32.6 0.1 broadcast_bitcast_fusion
  32.7 6.6 %copy.35 = f32[8,64,384]{0,2,1:T(8,128)} copy(f32[8,64,384]{2,1,0:T(8,128)S(1)} %fusion.11) | data formatting | bytes 1572864 | tf_op jit(solution)/shard_map/sub | solution.py:63
  39.2 5.6 %gather_fusion = f32[512,8]{1,0:T(8,128)S(1)} fusion(f32[8,24576]{0,1:T(8,128)} %bitcast.25, s32[1024]{0:T(1024)S(1)} %pad_clamp_fusion), kind=kCustom, calls=%fused_computation | custom fusion | bytes 34816 | tf_op jit(solution)/shard_map/gather | solution.py:70
  44.9 0.2 multiply_reduce_fusion
  45.2 0.8 fusion.15
  46.1 14.6 %all_gather.14 = f32[64,128]{1,0:T(8,128)S(1)} all-gather(f32[8,128]{1,0:T(8,128)S(1)} %divide_bitcast_fusion), channel_id=1, replica_groups=mesh['mem'=8,'slab'=4] {'mem'}, dimensions={0}, use_global_device_ids=true | all-gather | bytes 36864 | tf_op jit(solution)/shard_map/all_gather | solution.py:76
  60.7 9.9 %all_gather.15 = f32[64,512]{1,0:T(8,128)S(1)} all-gather(f32[64,128]{1,0:T(8,128)S(1)} %broadcast_subtract_fusion), channel_id=1, replica_groups=mesh['mem'=8,'slab'=4] {'slab'}, dimensions={1}, use_global_device_ids=true | all-gather | bytes 163840 | tf_op jit(solution)/shard_map/all_gather | solution.py:85
  70.6 14.2 %all_gather.12 = f32[64,128]{1,0:T(8,128)S(1)} all-gather(f32[8,128]{1,0:T(8,128)} %reduce-scatter.2.cloned.1.call-done), channel_id=1, replica_groups=mesh['mem'=8,'slab'=4] {'mem'}, dimensions={0}, use_global_device_ids=true | all-gather | bytes 36864 | tf_op jit(solution)/shard_map/all_gather | solution.py:77
  84.7 9.0 %all_gather.13 = f32[64,512]{1,0:T(8,128)S(1)} all-gather(f32[64,128]{1,0:T(8,128)S(1)} %all_gather.12), channel_id=1, replica_groups=mesh['mem'=8,'slab'=4] {'slab'}, dimensions={1}, use_global_device_ids=true | all-gather | bytes 163840 | tf_op jit(solution)/shard_map/all_gather | solution.py:86
  93.8 5.2 %fusion.13 = f32[3072,512]{1,0:T(8,128)S(1)} fusion(f32[64,512]{1,0:T(8,128)S(1)} %all_gather.15, f32[8,8,3072]{2,0,1:T(8,128)S(1)} %all-to-all-done, f32[3072]{0:T(1024)S(1)} %broadcast_multiply_fusion), kind=kOutput, calls=%fused_computation.23 | convolution fusion | flops 1208156160 | bytes 7221248 | tf_op jit(solution)/shard_map/dot_general | solution.py:91
  99.0 6.0 %fusion.5 = f32[8,8,3072]{2,1,0:T(8,128)S(1)} fusion(f32[64,512]{1,0:T(8,128)S(1)} %all_gather.13, f32[3072,512]{1,0:T(8,128)S(1)} %fusion.13, f32[512]{0:T(512)S(1)} %broadcast_bitcast_fusion, f32[8,8,3072]{2,0,1:T(8,128)S(1)} %all-to-all-done), kind=kOutput, calls=%fused_computation.4 | convolution fusion | flops 1209729024 | bytes 7997440 | tf_op jit(solution)/shard_map/dot_general | solution.py:95
  105.1 25.4 %all_to_all.35 = f32[8,8,3072]{2,1,0:T(8,128)S(1)} all-to-all(f32[8,8,3072]{2,1,0:T(8,128)S(1)} %fusion.5), channel_id=1, replica_groups=mesh['mem'=8,'slab'=4] {'mem'}, dimensions={0} | all-to-all | bytes 1572864 | tf_op jit(solution)/shard_map/all_to_all | solution.py:99
  130.5 0.5 copy.39
  130.9 1.0 reshape.34
  (26 shorter events, 0.3 us)
Async XLA Ops:
  6.5 38.6 %copy-start = (f32[128,512]{1,0:T(8,128)S(1)}, f32[128,512]{1,0:T(8,128)}, u32[]{:S(2)}) copy-start(f32[128,512]{1,0:T(8,128)} %param.16) | copy-start | bytes 786436
  6.5 18.0 %copy-start.1 = (f32[8,64,384]{2,1,0:T(8,128)S(1)}, f32[8,64,384]{2,1,0:T(8,128)}, u32[]{:S(2)}) copy-start(f32[8,64,384]{2,1,0:T(8,128)} %param.9) | copy-start | bytes 2359300
  7.6 13.0 %collective-permute-start = (f32[9,2,384]{2,1,0:T(2,128)S(1)}, f32[9,2,384]{2,1,0:T(2,128)S(1)}, u32[]{:S(2)}, u32[]{:S(2)}) collective-permute-start(f32[9,2,384]{2,1,0:T(2,128)S(1)} %get-tuple-element.10), channel_id=1, source_target_pairs={{1,0},{2,1},{3,2},{5,4},{6,5},{7,6},{9,8},{10,9},{11,10},{13,12},{... | collective-permute-start | bytes 82952 | tf_op jit(solution)/shard_map/ppermute | solution.py:15
  8.9 12.6 %collective-permute-start.1 = (f32[9,2,384]{2,1,0:T(2,128)S(1)}, f32[9,2,384]{2,1,0:T(2,128)S(1)}, u32[]{:S(2)}, u32[]{:S(2)}) collective-permute-start(f32[9,2,384]{2,1,0:T(2,128)S(1)} %get-tuple-element.9), channel_id=1, source_target_pairs={{0,1},{1,2},{2,3},{4,5},{5,6},{6,7},{8,9},{9,10},{10,11},{12,13},{... | collective-permute-start | bytes 82952 | tf_op jit(solution)/shard_map/ppermute | solution.py:12
  23.2 9.3 %copy-start.2 = (s32[128,4]{0,1:T(4,128)S(1)}, s32[128,4]{0,1:T(4,128)}, u32[]{:S(2)}) copy-start(s32[128,4]{0,1:T(4,128)} %param.13) | copy-start | bytes 6148
  26.4 67.4 %all-to-all-start = ((f32[8,8,3072]{2,0,1:T(8,128)}), f32[8,8,3072]{2,0,1:T(8,128)S(1)}, u32[]{:S(2)}, u32[]{:S(2)}) async-start(f32[8,8,3072]{2,0,1:T(8,128)} %copy.34), calls=%async_computation | async-start | bytes 1572864 | tf_op jit(solution)/shard_map/all_to_all | solution.py:80
  31.8 38.8 %reduce-scatter.2.cloned.1.call-start = ((), (), s32[]{:S(2)}) async-start(), calls=%async_computation.3 | async-start | bytes 20480 | tf_op jit(solution)/shard_map/reduce_scatter | solution.py:74
  32.7 12.5 %copy-start.3 = (f32[8,128]{1,0:T(8,128)S(1)}, f32[8,128]{1,0:T(8,128)}, u32[]{:S(2)}) copy-start(f32[8,128]{1,0:T(8,128)} %param.15) | copy-start | bytes 12292
  32.7 12.5 %copy-start.4 = (f32[128]{0:T(128)S(1)}, f32[128]{0:T(128)}, u32[]{:S(2)}) copy-start(f32[128]{0:T(128)} %param.14) | copy-start | bytes 1540
Sparse Core Ops, SparseCore 0:
  46.2 24.1 reduce-scatter.1
where the time goes:
time: 139 us
  blocking collectives  73 us (53%)
  local copies, waits for them, and re-layouts  15.6 us (11%)
  between operations  13.6 us (10%)
  other arithmetic  12.3 us (9%)
  starting transfers between devices  12.2 us (9%)
  matrix products  12.1 us (9%)
    all_to_all x1, blocking collectives, local(): lax.all_to_all(analysis_cells, 'mem', split_axis=0, concat_axis=1, tiled=...  25.4 us
    all_gather x1, blocking collectives, local(): lax.all_gather(obs_model, 'mem', axis=0, tiled=True)  14.6 us
    all_gather x1, blocking collectives, local(): lax.all_gather(whitened, 'mem', axis=0, tiled=True)  14.2 us
    all_gather x1, blocking collectives, local(): lax.all_gather(obs_anomaly, 'slab', axis=1, tiled=True)  9.86 us
    all_gather x1, blocking collectives, local(): lax.all_gather(white_all, 'slab', axis=1, tiled=True)  9 us
    sub x1, local copies, waits for them, and re-layouts, local(): thickness - (column_fluxes[:, :, 1:] - column_fluxes[:, :, :-1])  6.56 us
    dot_general x1, matrix products, local(): lax.dot_general(white_full, tapered, (((1,), (1,)), ((), ())), precision=...  6.04 us
    gather x1, local copies, waits for them, and re-layouts, local(): picked = state_vector[:, local_cells]  5.6 us
  transfers between devices with their start and end apart: 4, of which 0 were waited for; matrix products, arithmetic and copies ran while one was open for 15% of the time, Pallas kernels for 0%

commit v1 on v0

--- a/solution.py
+++ b/solution.py
@@ -96,7 +96,19 @@
         white_full, tapered, (((1,), (1,)), ((), ())), precision=lax.Precision.HIGHEST
     )
     analysis_cells = cell_state + update
-    returned = lax.all_to_all(analysis_cells, "mem", split_axis=0, concat_axis=1, tiled=True)
+    ways, here = (lax.axis_size("mem"), lax.axis_index("mem"))
+    width_2 = analysis_cells.shape[0] // ways
+    dims = list(analysis_cells.shape)
+    dims[0] = width_2
+    height = dims[1]
+    dims[1] = height * ways
+    full = jnp.zeros(dims, analysis_cells.dtype)
+    for mask in range(ways):
+        part = lax.dynamic_slice_in_dim(analysis_cells, (here ^ mask) * width_2, width_2, axis=0)
+        if mask:
+            part = lax.ppermute(part, "mem", [(d, d ^ mask) for d in range(ways)])
+        full = lax.dynamic_update_slice_in_dim(full, part, (here ^ mask) * height, axis=1)
+    returned = full
     return returned.reshape(member_subset, band_rows, column_list)
 
 

time: 139 us -> 135 us (0.971)
  the two profiles are of different devices: /device:TPU:0 before, /device:TPU:17 now
where the time goes in v1:
time: 135 us; the launch traced here: 134 us
  blocking collectives  40.8 us (30%)
  starting transfers between devices  21.3 us (16%)
  waiting for transfers between devices  18.8 us (14%)
  local copies, waits for them, and re-layouts  15.4 us (11%)
  between operations  13.7 us (10%)
  other arithmetic  12.2 us (9%)
  matrix products  12.1 us (9%)
    ppermute x7, waiting for transfers between devices, local(): part = lax.ppermute(part, 'mem', [(d, d ^ mask) for d in range(ways)])  15.9 us
    all_gather x1, blocking collectives, local(): lax.all_gather(whitened, 'mem', axis=0, tiled=True)  13.5 us
    all_gather x1, blocking collectives, local(): lax.all_gather(obs_model, 'mem', axis=0, tiled=True)  12.5 us
    ppermute x7, starting transfers between devices, local(): part = lax.ppermute(part, 'mem', [(d, d ^ mask) for d in range(ways)])  9.99 us
    all_gather x1, blocking collectives, local(): lax.all_gather(obs_anomaly, 'slab', axis=1, tiled=True)  7.83 us
    all_gather x1, blocking collectives, local(): lax.all_gather(white_all, 'slab', axis=1, tiled=True)  6.98 us
    sub x1, local copies, waits for them, and re-layouts, local(): thickness - (column_fluxes[:, :, 1:] - column_fluxes[:, :, :-1])  6.59 us
    all_to_all x1, starting transfers between devices, local(): lax.all_to_all(state_vector, 'mem', split_axis=1, concat_axis=0, tiled=True)  6.05 us
  transfers between devices with their start and end apart: 11, of which 6 were waited for; matrix products, arithmetic and copies ran while one was open for 16% of the time, Pallas kernels for 0%

profile of v1, /device:TPU:17, one launch (start us, length us, event | category | flops | bytes accessed | tf_op | source)
XLA Modules:
  0.0 134.3 jit_solution(2671326513478042009)
XLA Ops:
  6.5 1.1 pad_maximum_fusion.3
  7.6 1.3 collective-permute-start
  8.9 4.0 %collective-permute-start.1 = (f32[9,2,384]{2,1,0:T(2,128)S(1)}, f32[9,2,384]{2,1,0:T(2,128)S(1)}, u32[]{:S(2)}, u32[]{:S(2)}) collective-permute-start(f32[9,2,384]{2,1,0:T(2,128)S(1)} %get-tuple-element.9), channel_id=1, source_target_pairs={{0,1},{1,2},{2,3},{4,5},{5,6},{6,7},{8,9},{9,10},{10,11},{12,13},{... | collective-permute-start | bytes 82952 | tf_op jit(solution)/shard_map/ppermute | solution.py:12
  12.9 0.9 pad_maximum_fusion.1
  14.8 3.6 %multiply_add_fusion = f32[8,64,385]{2,1,0:T(8,128)S(1)} fusion(f32[8,64,384]{2,1,0:T(8,128)} %param.9, f32[64,385]{1,0:T(8,128)S(1)} %get-tuple-element.20, f32[64,385]{1,0:T(8,128)S(1)} %get-tuple-element.19), kind=kLoop, calls=%fused_computation.11 | loop fusion | flops 4730880 | bytes 1772032 | tf_op jit(solution)/shard_map/add | solution.py:36
  18.4 0.7 convert_reduce_fusion
  19.1 0.9 maximum_bitcast_fusion
  20.1 1.6 %maximum_maximum_fusion = (f32[9,66,384]{2,1,0:T(8,128)S(1)}, f32[9,66,384]{2,1,0:T(8,128)S(1)}) fusion(f32[1,64,384]{2,1,0:T(8,128)} %bitcast.31, f32[8,64,384]{2,1,0:T(8,128)} %param.9, f32[9,2,384]{2,1,0:T(2,128)S(1)} %collective-permute-done.1, f32[9,2,384]{2,1,0:T(2,128)S(1)} %collective-permute-done), kind=kLoop, calls=%fused_computation.13 | loop fusion | flops 912384 | bytes 2764800 | tf_op jit(solution)/shard_map/concatenate | solution.py:16
  21.7 1.3 multiply_add_fusion.1
  23.5 1.3 copy.30
  24.8 6.1 %all-to-all-start = ((f32[8,8,3072]{2,0,1:T(8,128)}), f32[8,8,3072]{2,0,1:T(8,128)S(1)}, u32[]{:S(2)}, u32[]{:S(2)}) async-start(f32[8,8,3072]{2,0,1:T(8,128)} %copy.30), calls=%async_computation | async-start | bytes 1572864 | tf_op jit(solution)/shard_map/all_to_all | solution.py:80
  31.8 6.6 %copy.31 = f32[8,64,384]{0,2,1:T(8,128)} copy(f32[8,64,384]{2,1,0:T(8,128)S(1)} %fusion.8) | data formatting | bytes 1572864 | tf_op jit(solution)/shard_map/sub | solution.py:63
  38.4 5.6 %gather_fusion = f32[512,8]{1,0:T(8,128)S(1)} fusion(f32[8,24576]{0,1:T(8,128)} %bitcast.26, s32[1024]{0:T(1024)S(1)} %pad_clamp_fusion), kind=kCustom, calls=%fused_computation | custom fusion | bytes 34816 | tf_op jit(solution)/shard_map/gather | solution.py:70
  44.4 0.8 fusion.12
  45.2 12.5 %all_gather.14 = f32[64,128]{1,0:T(8,128)S(1)} all-gather(f32[8,128]{1,0:T(8,128)S(1)} %divide_bitcast_fusion), channel_id=1, replica_groups=mesh['mem'=8,'slab'=4] {'mem'}, dimensions={0}, use_global_device_ids=true | all-gather | bytes 36864 | tf_op jit(solution)/shard_map/all_gather | solution.py:76
  57.8 7.8 %all_gather.15 = f32[64,512]{1,0:T(8,128)S(1)} all-gather(f32[64,128]{1,0:T(8,128)S(1)} %broadcast_subtract_fusion), channel_id=1, replica_groups=mesh['mem'=8,'slab'=4] {'slab'}, dimensions={1}, use_global_device_ids=true | all-gather | bytes 163840 | tf_op jit(solution)/shard_map/all_gather | solution.py:85
  65.6 2.9 %reduce-scatter.2.cloned.1.call-done = f32[8,128]{1,0:T(8,128)} async-done(((f32[8,512]{1,0:T(8,128)}), f32[8,128]{1,0:T(8,128)}) %reduce-scatter.2.cloned.1.call-update) | async-done | bytes 4112 | tf_op jit(solution)/shard_map/reduce_scatter | solution.py:74
  68.5 13.5 %all_gather.12 = f32[64,128]{1,0:T(8,128)S(1)} all-gather(f32[8,128]{1,0:T(8,128)} %reduce-scatter.2.cloned.1.call-done), channel_id=1, replica_groups=mesh['mem'=8,'slab'=4] {'mem'}, dimensions={0}, use_global_device_ids=true | all-gather | bytes 36864 | tf_op jit(solution)/shard_map/all_gather | solution.py:77
  82.0 7.0 %all_gather.13 = f32[64,512]{1,0:T(8,128)S(1)} all-gather(f32[64,128]{1,0:T(8,128)S(1)} %all_gather.12), channel_id=1, replica_groups=mesh['mem'=8,'slab'=4] {'slab'}, dimensions={1}, use_global_device_ids=true | all-gather | bytes 163840 | tf_op jit(solution)/shard_map/all_gather | solution.py:86
  89.0 5.2 %fusion.10 = f32[3072,512]{1,0:T(8,128)S(1)} fusion(f32[64,512]{1,0:T(8,128)S(1)} %all_gather.15, f32[8,8,3072]{2,0,1:T(8,128)S(1)} %all-to-all-done, f32[3072]{0:T(1024)S(1)} %broadcast_multiply_fusion), kind=kOutput, calls=%fused_computation.23 | convolution fusion | flops 1208156160 | bytes 7221248 | tf_op jit(solution)/shard_map/dot_general | solution.py:91
  94.2 6.0 %fusion.2 = f32[64,3072]{1,0:T(8,128)S(1)} fusion(f32[64,512]{1,0:T(8,128)S(1)} %all_gather.13, f32[3072,512]{1,0:T(8,128)S(1)} %fusion.10, f32[512]{0:T(512)S(1)} %broadcast_bitcast_fusion, f32[8,8,3072]{2,0,1:T(8,128)S(1)} %all-to-all-done), kind=kOutput, calls=%fused_computation.3 | convolution fusion | flops 1209729024 | bytes 7997440 | tf_op jit(solution)/shard_map/dot_general | solution.py:95
  100.4 2.3 %collective-permute-start.2 = (f32[8,3072]{1,0:T(8,128)S(1)}, f32[8,3072]{1,0:T(8,128)S(1)}, u32[]{:S(2)}, u32[]{:S(2)}) collective-permute-start(f32[8,3072]{1,0:T(8,128)S(1)} %get-tuple-element.17), channel_id=1, source_target_pairs={{0,4},{4,0},{8,12},{12,8},{16,20},{20,16},{24,28},{28,24},{1,5},{5... | collective-permute-start | bytes 294920 | tf_op jit(solution)/shard_map/ppermute | solution.py:109
  102.7 3.0 %collective-permute-start.3 = (f32[8,3072]{1,0:T(8,128)S(1)}, f32[8,3072]{1,0:T(8,128)S(1)}, u32[]{:S(2)}, u32[]{:S(2)}) collective-permute-start(f32[8,3072]{1,0:T(8,128)S(1)} %get-tuple-element.16), channel_id=1, source_target_pairs={{0,8},{4,12},{8,0},{12,4},{16,24},{20,28},{24,16},{28,20},{1,9},{5... | collective-permute-start | bytes 294920 | tf_op jit(solution)/shard_map/ppermute | solution.py:109
  105.7 0.8 collective-permute-start.5
  106.5 2.1 %collective-permute-start.6 = (f32[8,3072]{1,0:T(8,128)S(1)}, f32[8,3072]{1,0:T(8,128)S(1)}, u32[]{:S(2)}, u32[]{:S(2)}) collective-permute-start(f32[8,3072]{1,0:T(8,128)S(1)} %get-tuple-element.13), channel_id=1, source_target_pairs={{0,20},{4,16},{8,28},{12,24},{16,4},{20,0},{24,12},{28,8},{1,21},{... | collective-permute-start | bytes 294920 | tf_op jit(solution)/shard_map/ppermute | solution.py:109
  109.2 1.3 collective-permute-start.8
  110.4 0.7 collective-permute-done.4
  111.2 1.7 %collective-permute-done.5 = f32[8,3072]{1,0:T(8,128)S(1)} collective-permute-done((f32[8,3072]{1,0:T(8,128)S(1)}, f32[8,3072]{1,0:T(8,128)S(1)}, u32[]{:S(2)}, u32[]{:S(2)}) %collective-permute-start.5) | collective-permute-done | bytes 98336 | tf_op jit(solution)/shard_map/ppermute | solution.py:109
  112.9 6.7 %collective-permute-done.6 = f32[8,3072]{1,0:T(8,128)S(1)} collective-permute-done((f32[8,3072]{1,0:T(8,128)S(1)}, f32[8,3072]{1,0:T(8,128)S(1)}, u32[]{:S(2)}, u32[]{:S(2)}) %collective-permute-start.6) | collective-permute-done | bytes 98336 | tf_op jit(solution)/shard_map/ppermute | solution.py:109
  119.6 4.4 %collective-permute-done.7 = f32[8,3072]{1,0:T(8,128)S(1)} collective-permute-done((f32[8,3072]{1,0:T(8,128)S(1)}, f32[8,3072]{1,0:T(8,128)S(1)}, u32[]{:S(2)}, u32[]{:S(2)}) %collective-permute-start.7) | collective-permute-done | bytes 98336 | tf_op jit(solution)/shard_map/ppermute | solution.py:109
  124.0 2.4 %collective-permute-done.8 = f32[8,3072]{1,0:T(8,128)S(1)} collective-permute-done((f32[8,3072]{1,0:T(8,128)S(1)}, f32[8,3072]{1,0:T(8,128)S(1)}, u32[]{:S(2)}, u32[]{:S(2)}) %collective-permute-start.8) | collective-permute-done | bytes 98336 | tf_op jit(solution)/shard_map/ppermute | solution.py:109
  126.4 1.0 copy.37
  (47 shorter events, 3.5 us)
Async XLA Ops:
  6.5 37.8 %copy-start = (f32[128,512]{1,0:T(8,128)S(1)}, f32[128,512]{1,0:T(8,128)}, u32[]{:S(2)}) copy-start(f32[128,512]{1,0:T(8,128)} %param.16) | copy-start | bytes 786436
  6.5 16.5 %copy-start.1 = (f32[8,64,384]{2,1,0:T(8,128)S(1)}, f32[8,64,384]{2,1,0:T(8,128)}, u32[]{:S(2)}) copy-start(f32[8,64,384]{2,1,0:T(8,128)} %param.9) | copy-start | bytes 2359300
  7.6 11.5 %collective-permute-start = (f32[9,2,384]{2,1,0:T(2,128)S(1)}, f32[9,2,384]{2,1,0:T(2,128)S(1)}, u32[]{:S(2)}, u32[]{:S(2)}) collective-permute-start(f32[9,2,384]{2,1,0:T(2,128)S(1)} %get-tuple-element.10), channel_id=1, source_target_pairs={{1,0},{2,1},{3,2},{5,4},{6,5},{7,6},{9,8},{10,9},{11,10},{13,12},{... | collective-permute-start | bytes 82952 | tf_op jit(solution)/shard_map/ppermute | solution.py:15
  8.9 11.1 %collective-permute-start.1 = (f32[9,2,384]{2,1,0:T(2,128)S(1)}, f32[9,2,384]{2,1,0:T(2,128)S(1)}, u32[]{:S(2)}, u32[]{:S(2)}) collective-permute-start(f32[9,2,384]{2,1,0:T(2,128)S(1)} %get-tuple-element.9), channel_id=1, source_target_pairs={{0,1},{1,2},{2,3},{4,5},{5,6},{6,7},{8,9},{9,10},{10,11},{12,13},{... | collective-permute-start | bytes 82952 | tf_op jit(solution)/shard_map/ppermute | solution.py:12
  21.7 9.9 %copy-start.2 = (s32[128,4]{0,1:T(4,128)S(1)}, s32[128,4]{0,1:T(4,128)}, u32[]{:S(2)}) copy-start(s32[128,4]{0,1:T(4,128)} %param.13) | copy-start | bytes 6148
  24.8 64.1 %all-to-all-start = ((f32[8,8,3072]{2,0,1:T(8,128)}), f32[8,8,3072]{2,0,1:T(8,128)S(1)}, u32[]{:S(2)}, u32[]{:S(2)}) async-start(f32[8,8,3072]{2,0,1:T(8,128)} %copy.30), calls=%async_computation | async-start | bytes 1572864 | tf_op jit(solution)/shard_map/all_to_all | solution.py:80
  30.9 37.6 %reduce-scatter.2.cloned.1.call-start = ((), (), s32[]{:S(2)}) async-start(), calls=%async_computation.2 | async-start | bytes 20480 | tf_op jit(solution)/shard_map/reduce_scatter | solution.py:74
  31.8 12.5 %copy-start.3 = (f32[8,128]{1,0:T(8,128)S(1)}, f32[8,128]{1,0:T(8,128)}, u32[]{:S(2)}) copy-start(f32[8,128]{1,0:T(8,128)} %param.15) | copy-start | bytes 12292
  31.8 12.5 %copy-start.4 = (f32[128]{0:T(128)S(1)}, f32[128]{0:T(128)}, u32[]{:S(2)}) copy-start(f32[128]{0:T(128)} %param.14) | copy-start | bytes 1540
  100.4 8.2 %collective-permute-start.2 = (f32[8,3072]{1,0:T(8,128)S(1)}, f32[8,3072]{1,0:T(8,128)S(1)}, u32[]{:S(2)}, u32[]{:S(2)}) collective-permute-start(f32[8,3072]{1,0:T(8,128)S(1)} %get-tuple-element.17), channel_id=1, source_target_pairs={{0,4},{4,0},{8,12},{12,8},{16,20},{20,16},{24,28},{28,24},{1,5},{5... | collective-permute-start | bytes 294920 | tf_op jit(solution)/shard_map/ppermute | solution.py:109
  102.7 6.5 %collective-permute-start.3 = (f32[8,3072]{1,0:T(8,128)S(1)}, f32[8,3072]{1,0:T(8,128)S(1)}, u32[]{:S(2)}, u32[]{:S(2)}) collective-permute-start(f32[8,3072]{1,0:T(8,128)S(1)} %get-tuple-element.16), channel_id=1, source_target_pairs={{0,8},{4,12},{8,0},{12,4},{16,24},{20,28},{24,16},{28,20},{1,9},{5... | collective-permute-start | bytes 294920 | tf_op jit(solution)/shard_map/ppermute | solution.py:109
  105.6 5.5 %collective-permute-start.4 = (f32[8,3072]{1,0:T(8,128)S(1)}, f32[8,3072]{1,0:T(8,128)S(1)}, u32[]{:S(2)}, u32[]{:S(2)}) collective-permute-start(f32[8,3072]{1,0:T(8,128)S(1)} %get-tuple-element.15), channel_id=1, source_target_pairs={{0,12},{4,8},{8,4},{12,0},{16,28},{20,24},{24,20},{28,16},{1,13},{... | collective-permute-start | bytes 294920 | tf_op jit(solution)/shard_map/ppermute | solution.py:109
  105.7 7.2 %collective-permute-start.5 = (f32[8,3072]{1,0:T(8,128)S(1)}, f32[8,3072]{1,0:T(8,128)S(1)}, u32[]{:S(2)}, u32[]{:S(2)}) collective-permute-start(f32[8,3072]{1,0:T(8,128)S(1)} %get-tuple-element.14), channel_id=1, source_target_pairs={{0,16},{4,20},{8,24},{12,28},{16,0},{20,4},{24,8},{28,12},{1,17},{... | collective-permute-start | bytes 294920 | tf_op jit(solution)/shard_map/ppermute | solution.py:109
  106.5 13.1 %collective-permute-start.6 = (f32[8,3072]{1,0:T(8,128)S(1)}, f32[8,3072]{1,0:T(8,128)S(1)}, u32[]{:S(2)}, u32[]{:S(2)}) collective-permute-start(f32[8,3072]{1,0:T(8,128)S(1)} %get-tuple-element.13), channel_id=1, source_target_pairs={{0,20},{4,16},{8,28},{12,24},{16,4},{20,0},{24,12},{28,8},{1,21},{... | collective-permute-start | bytes 294920 | tf_op jit(solution)/shard_map/ppermute | solution.py:109
  108.6 15.4 %collective-permute-start.7 = (f32[8,3072]{1,0:T(8,128)S(1)}, f32[8,3072]{1,0:T(8,128)S(1)}, u32[]{:S(2)}, u32[]{:S(2)}) collective-permute-start(f32[8,3072]{1,0:T(8,128)S(1)} %get-tuple-element.12), channel_id=1, source_target_pairs={{0,24},{4,28},{8,16},{12,20},{16,8},{20,12},{24,0},{28,4},{1,25},{... | collective-permute-start | bytes 294920 | tf_op jit(solution)/shard_map/ppermute | solution.py:109
  109.2 17.2 %collective-permute-start.8 = (f32[8,3072]{1,0:T(8,128)S(1)}, f32[8,3072]{1,0:T(8,128)S(1)}, u32[]{:S(2)}, u32[]{:S(2)}) collective-permute-start(f32[8,3072]{1,0:T(8,128)S(1)} %get-tuple-element.11), channel_id=1, source_target_pairs={{0,28},{4,24},{8,20},{12,16},{16,12},{20,8},{24,4},{28,0},{1,29},{... | collective-permute-start | bytes 294920 | tf_op jit(solution)/shard_map/ppermute | solution.py:109
Sparse Core Ops, SparseCore 0:
  45.4 23.1 reduce-scatter.1
